TPU v7x, 32 devices: a whole 2x2x4 slice. The times are simulated.
32 devices in a mesh: dp: 4 (over x, core), enc: 8 (over z, y).
Axes of the slice: x: 2, y: 2, z: 4, core: 2. Of those that a mesh axis runs over, the one named last changes fastest.
Arguments:
- hidden_states: bfloat16 [2048, 4096], P('dp', 'enc'), as said below
- dec_gain: bfloat16 [4096], replicated, as said below
- nbr_tokens: bfloat16 [48, 128, 4096], P('dp', 'enc'), as said below
- enc_gain: bfloat16 [4096], replicated, as said below
- query_weight: bfloat16 [4096, 4096], P(None, 'enc'), may hold values from -0.09375 to 0.09375
- key_weight: bfloat16 [4096, 4096], P(None, 'enc'), may hold values from -0.09375 to 0.09375
- value_weight: bfloat16 [4096, 4096], P(None, 'enc'), may hold values from -0.09375 to 0.09375
- out_weight: bfloat16 [4096, 4096], P('enc'), may hold values from -0.09375 to 0.09375
- cite_owner: int32 [64, 1], P('dp'), may hold values from 0 to 3; in each aligned block of 16 rows (0 to 15, 16 to 31, ...) at most 8 rows name the same one
- cite_local: int32 [32, 2], P('dp'), may hold values from 0 to 11
Outputs:
- block_out: bfloat16 [2048, 4096], P(('dp', 'enc'))
Inputs may be any that keep to these rules, and one draw needn't show every extreme that they name: `cite_owner`: among the citations of one index of dp, no owner is named more than 8 times, a bound that some block reaches. `hidden_states`: token rows have widely differing magnitudes. `nbr_tokens`: token rows have widely differing magnitudes. `dec_gain`: Positive. `enc_gain`: Positive.
All inputs are finite; a program needn't handle non-finite values.
Results may differ from a plain program's by a relative error of at most 0.013.
The roundings to bfloat16 on the way count: a program that leaves them out, or rounds other values in their place, can miss the bound.
Values may be sent and summed in bfloat16 or wider, within the bound.
A program may use at most 128 MiB of HBM per device.

v0:
```python
import jax
import jax.numpy as jnp
from jax import lax
from jax.sharding import PartitionSpec as P

HD = 128
SPAN = 64
NL = 128
NBRS = 2


def normalize(rows, gain):
    values = rows.astype(jnp.float32)
    scale = lax.rsqrt(jnp.mean(values * values, axis=-1, keepdims=True) + 1e-05)
    return (values * scale * gain.astype(jnp.float32)).astype(jnp.bfloat16)


def per_device(
    hidden_states,
    dec_gain,
    nbr_tokens,
    enc_gain,
    query_weight,
    key_weight,
    value_weight,
    out_weight,
    cite_owner,
    cite_local,
):
    kv_weight = jnp.concatenate((key_weight, value_weight), axis=1)

    def encode_tile(tile):
        return jnp.dot(
            normalize(tile, enc_gain), kv_weight, preferred_element_type=jnp.float32
        ).astype(jnp.bfloat16)

    encoded = lax.map(encode_tile, lax.all_gather(nbr_tokens, "enc", axis=1, tiled=True))
    whole = lax.all_gather(hidden_states, "enc", axis=1, tiled=True)
    queries = jnp.dot(
        normalize(whole, dec_gain), query_weight, preferred_element_type=jnp.float32
    ).astype(jnp.bfloat16)
    tok_rows = whole.shape[0]
    width = queries.shape[1]
    heads_here = width // HD
    span_count = tok_rows // SPAN
    owners = cite_owner[:, 0]
    tile_local = cite_local.reshape(-1)
    tiles_dev = encoded.shape[0]
    tile_ids = owners * tiles_dev + tile_local
    empty = jnp.zeros((owners.shape[0],) + encoded.shape[1:], jnp.bfloat16)
    piece = lax.all_gather(encoded, "dp", axis=0, tiled=True)
    count = piece.shape[0]
    inside = (tile_ids >= 0) & (tile_ids < count)
    picked = jnp.take(piece, jnp.clip(tile_ids, 0, count - 1), axis=0)
    cited = jnp.where(inside[:, None, None], picked, empty)
    kv = cited.reshape(span_count, NBRS * NL, 2, heads_here, HD)
    query_blocks = queries.reshape(span_count, SPAN, heads_here, HD)
    scores = jnp.einsum(
        "cqhd,ckhd->chqk", query_blocks, kv[:, :, 0], preferred_element_type=jnp.float32
    ) * HD ** (-0.5)
    weights = jax.nn.softmax(scores, axis=-1).astype(jnp.bfloat16)
    context = jnp.einsum(
        "chqk,ckhd->cqhd", weights, kv[:, :, 1], preferred_element_type=jnp.float32
    )
    context = context.astype(jnp.bfloat16).reshape(tok_rows, width)
    return lax.psum_scatter(
        jnp.dot(context, out_weight, preferred_element_type=jnp.float32).astype(jnp.bfloat16),
        "enc",
        scatter_dimension=0,
        tiled=True,
    )


def solution(mesh):
    in_specs = (
        P("dp", "enc"),
        P(),
        P("dp", "enc", None),
        P(),
        P(None, "enc"),
        P(None, "enc"),
        P(None, "enc"),
        P("enc", None),
        P("dp", None),
        P("dp", None),
    )
    out_specs = P(("dp", "enc"), None)
    return jax.shard_map(
        per_device, mesh=mesh, in_specs=in_specs, out_specs=out_specs, check_vma=False
    )
```

profile of v0, /device:TPU:0, one launch (start us, length us, event | category | flops | bytes accessed | tf_op | source)
XLA Modules:
  0.0 485.8 jit_solution(11635320714324521103)
XLA Ops:
  8.1 7.8 %pad_maximum_fusion = bf16[4096,1024]{1,0:T(8,128)(2,1)} fusion(bf16[4096,512]{1,0:T(8,128)(2,1)} %param.18, bf16[4096,512]{1,0:T(8,128)(2,1)} %param.17), kind=kLoop, calls=%fused_computation.21 | loop fusion | flops 16777216 | bytes 16777216 | tf_op jit(solution)/shard_map/concatenate | solution.py:30
  15.9 172.5 %all-gather.4.cloned.1.call-done = bf16[12,128,4096]{2,1,0:T(8,128)(2,1)} async-done(((bf16[12,16,4096]{2,1,0:T(8,128)(2,1)}), bf16[12,128,4096]{2,1,0:T(8,128)(2,1)}) %all-gather.4.cloned.1.call-update) | async-done | bytes 12582928 | tf_op jit(solution)/shard_map/all_gather | solution.py:37
  188.4 87.9 %while.10 = (s32[]{:T(128)}, bf16[12,128,1024]{2,1,0:T(8,128)(2,1)}, bf16[12,128,4096]{2,1,0:T(8,128)(2,1)}, bf16[4096]{0:T(1024)(128)(2,1)S(1)}, bf16[4096,1024]{1,0:T(8,128)(2,1)}, /*index=5*/s32[]{:T(128)}) while((s32[]{:T(128)}, bf16[12,128,1024]{2,1,0:T(8,128)(2,1)}, bf16[12,128,4096]{2,1,0:T(8,128)(2,1)}, bf16[4096]{0:T(1024)(128)(2,1)S(1)}, ...), condition=%wide.region_2.3_spmd, body=%wide.region_0.2_spmd.sunk | while | flops 1077547136 | bytes 10792017 | solution.py:37
  189.9 5.7 %fusion.52 = bf16[12,128,1024]{2,1,0:T(8,128)(2,1)} fusion(bf16[12,128,1024]{2,1,0:T(8,128)(2,1)} %get-tuple-element.85, s32[]{:T(128)S(6)} %copy.47, bf16[4096,1024]{1,0:T(8,128)(2,1)} %get-tuple-element.94, f32[4096]{0:T(1024)S(1)} %convert_element_type.86, f32[128]{0:T(128)S(1)} %add_rsqrt_fusion.3, bf16[12,128,4096]{2,1,0:T(8,128)(2,1)} %get-tuple-element.92), kind=kOutput, calls=%fused_computation.8.clone.1 | convolution fusion | flops 1075970048 | bytes 9717248 | tf_op jit(solution)/shard_map/while/body/eval_jaxpr/dot_general | solution.py:33
  197.3 5.8 %fusion.52 = bf16[12,128,1024]{2,1,0:T(8,128)(2,1)} fusion(bf16[12,128,1024]{2,1,0:T(8,128)(2,1)} %get-tuple-element.85, s32[]{:T(128)S(6)} %copy.47, bf16[4096,1024]{1,0:T(8,128)(2,1)} %get-tuple-element.94, f32[4096]{0:T(1024)S(1)} %convert_element_type.86, f32[128]{0:T(128)S(1)} %add_rsqrt_fusion.3, bf16[12,128,4096]{2,1,0:T(8,128)(2,1)} %get-tuple-element.92), kind=kOutput, calls=%fused_computation.8.clone.1 | convolution fusion | flops 1075970048 | bytes 9717248 | tf_op jit(solution)/shard_map/while/body/eval_jaxpr/dot_general | solution.py:33
  204.7 5.8 %fusion.52 = bf16[12,128,1024]{2,1,0:T(8,128)(2,1)} fusion(bf16[12,128,1024]{2,1,0:T(8,128)(2,1)} %get-tuple-element.85, s32[]{:T(128)S(6)} %copy.47, bf16[4096,1024]{1,0:T(8,128)(2,1)} %get-tuple-element.94, f32[4096]{0:T(1024)S(1)} %convert_element_type.86, f32[128]{0:T(128)S(1)} %add_rsqrt_fusion.3, bf16[12,128,4096]{2,1,0:T(8,128)(2,1)} %get-tuple-element.92), kind=kOutput, calls=%fused_computation.8.clone.1 | convolution fusion | flops 1075970048 | bytes 9717248 | tf_op jit(solution)/shard_map/while/body/eval_jaxpr/dot_general | solution.py:33
  212.0 5.8 %fusion.52 = bf16[12,128,1024]{2,1,0:T(8,128)(2,1)} fusion(bf16[12,128,1024]{2,1,0:T(8,128)(2,1)} %get-tuple-element.85, s32[]{:T(128)S(6)} %copy.47, bf16[4096,1024]{1,0:T(8,128)(2,1)} %get-tuple-element.94, f32[4096]{0:T(1024)S(1)} %convert_element_type.86, f32[128]{0:T(128)S(1)} %add_rsqrt_fusion.3, bf16[12,128,4096]{2,1,0:T(8,128)(2,1)} %get-tuple-element.92), kind=kOutput, calls=%fused_computation.8.clone.1 | convolution fusion | flops 1075970048 | bytes 9717248 | tf_op jit(solution)/shard_map/while/body/eval_jaxpr/dot_general | solution.py:33
  219.3 5.7 %fusion.52 = bf16[12,128,1024]{2,1,0:T(8,128)(2,1)} fusion(bf16[12,128,1024]{2,1,0:T(8,128)(2,1)} %get-tuple-element.85, s32[]{:T(128)S(6)} %copy.47, bf16[4096,1024]{1,0:T(8,128)(2,1)} %get-tuple-element.94, f32[4096]{0:T(1024)S(1)} %convert_element_type.86, f32[128]{0:T(128)S(1)} %add_rsqrt_fusion.3, bf16[12,128,4096]{2,1,0:T(8,128)(2,1)} %get-tuple-element.92), kind=kOutput, calls=%fused_computation.8.clone.1 | convolution fusion | flops 1075970048 | bytes 9717248 | tf_op jit(solution)/shard_map/while/body/eval_jaxpr/dot_general | solution.py:33
  226.6 5.9 %fusion.52 = bf16[12,128,1024]{2,1,0:T(8,128)(2,1)} fusion(bf16[12,128,1024]{2,1,0:T(8,128)(2,1)} %get-tuple-element.85, s32[]{:T(128)S(6)} %copy.47, bf16[4096,1024]{1,0:T(8,128)(2,1)} %get-tuple-element.94, f32[4096]{0:T(1024)S(1)} %convert_element_type.86, f32[128]{0:T(128)S(1)} %add_rsqrt_fusion.3, bf16[12,128,4096]{2,1,0:T(8,128)(2,1)} %get-tuple-element.92), kind=kOutput, calls=%fused_computation.8.clone.1 | convolution fusion | flops 1075970048 | bytes 9717248 | tf_op jit(solution)/shard_map/while/body/eval_jaxpr/dot_general | solution.py:33
  234.0 5.8 %fusion.52 = bf16[12,128,1024]{2,1,0:T(8,128)(2,1)} fusion(bf16[12,128,1024]{2,1,0:T(8,128)(2,1)} %get-tuple-element.85, s32[]{:T(128)S(6)} %copy.47, bf16[4096,1024]{1,0:T(8,128)(2,1)} %get-tuple-element.94, f32[4096]{0:T(1024)S(1)} %convert_element_type.86, f32[128]{0:T(128)S(1)} %add_rsqrt_fusion.3, bf16[12,128,4096]{2,1,0:T(8,128)(2,1)} %get-tuple-element.92), kind=kOutput, calls=%fused_computation.8.clone.1 | convolution fusion | flops 1075970048 | bytes 9717248 | tf_op jit(solution)/shard_map/while/body/eval_jaxpr/dot_general | solution.py:33
  241.4 5.7 %fusion.52 = bf16[12,128,1024]{2,1,0:T(8,128)(2,1)} fusion(bf16[12,128,1024]{2,1,0:T(8,128)(2,1)} %get-tuple-element.85, s32[]{:T(128)S(6)} %copy.47, bf16[4096,1024]{1,0:T(8,128)(2,1)} %get-tuple-element.94, f32[4096]{0:T(1024)S(1)} %convert_element_type.86, f32[128]{0:T(128)S(1)} %add_rsqrt_fusion.3, bf16[12,128,4096]{2,1,0:T(8,128)(2,1)} %get-tuple-element.92), kind=kOutput, calls=%fused_computation.8.clone.1 | convolution fusion | flops 1075970048 | bytes 9717248 | tf_op jit(solution)/shard_map/while/body/eval_jaxpr/dot_general | solution.py:33
  248.6 5.9 %fusion.52 = bf16[12,128,1024]{2,1,0:T(8,128)(2,1)} fusion(bf16[12,128,1024]{2,1,0:T(8,128)(2,1)} %get-tuple-element.85, s32[]{:T(128)S(6)} %copy.47, bf16[4096,1024]{1,0:T(8,128)(2,1)} %get-tuple-element.94, f32[4096]{0:T(1024)S(1)} %convert_element_type.86, f32[128]{0:T(128)S(1)} %add_rsqrt_fusion.3, bf16[12,128,4096]{2,1,0:T(8,128)(2,1)} %get-tuple-element.92), kind=kOutput, calls=%fused_computation.8.clone.1 | convolution fusion | flops 1075970048 | bytes 9717248 | tf_op jit(solution)/shard_map/while/body/eval_jaxpr/dot_general | solution.py:33
  256.0 5.7 %fusion.52 = bf16[12,128,1024]{2,1,0:T(8,128)(2,1)} fusion(bf16[12,128,1024]{2,1,0:T(8,128)(2,1)} %get-tuple-element.85, s32[]{:T(128)S(6)} %copy.47, bf16[4096,1024]{1,0:T(8,128)(2,1)} %get-tuple-element.94, f32[4096]{0:T(1024)S(1)} %convert_element_type.86, f32[128]{0:T(128)S(1)} %add_rsqrt_fusion.3, bf16[12,128,4096]{2,1,0:T(8,128)(2,1)} %get-tuple-element.92), kind=kOutput, calls=%fused_computation.8.clone.1 | convolution fusion | flops 1075970048 | bytes 9717248 | tf_op jit(solution)/shard_map/while/body/eval_jaxpr/dot_general | solution.py:33
  263.3 5.7 %fusion.52 = bf16[12,128,1024]{2,1,0:T(8,128)(2,1)} fusion(bf16[12,128,1024]{2,1,0:T(8,128)(2,1)} %get-tuple-element.85, s32[]{:T(128)S(6)} %copy.47, bf16[4096,1024]{1,0:T(8,128)(2,1)} %get-tuple-element.94, f32[4096]{0:T(1024)S(1)} %convert_element_type.86, f32[128]{0:T(128)S(1)} %add_rsqrt_fusion.3, bf16[12,128,4096]{2,1,0:T(8,128)(2,1)} %get-tuple-element.92), kind=kOutput, calls=%fused_computation.8.clone.1 | convolution fusion | flops 1075970048 | bytes 9717248 | tf_op jit(solution)/shard_map/while/body/eval_jaxpr/dot_general | solution.py:33
  270.6 5.7 %fusion.52 = bf16[12,128,1024]{2,1,0:T(8,128)(2,1)} fusion(bf16[12,128,1024]{2,1,0:T(8,128)(2,1)} %get-tuple-element.85, s32[]{:T(128)S(6)} %copy.47, bf16[4096,1024]{1,0:T(8,128)(2,1)} %get-tuple-element.94, f32[4096]{0:T(1024)S(1)} %convert_element_type.86, f32[128]{0:T(128)S(1)} %add_rsqrt_fusion.3, bf16[12,128,4096]{2,1,0:T(8,128)(2,1)} %get-tuple-element.92), kind=kOutput, calls=%fused_computation.8.clone.1 | convolution fusion | flops 1075970048 | bytes 9717248 | tf_op jit(solution)/shard_map/while/body/eval_jaxpr/dot_general | solution.py:33
  277.3 3.2 fusion.12
  280.7 5.2 %fusion.24 = bf16[512,512]{1,0:T(8,128)(2,1)S(1)} fusion(bf16[4096,512]{1,0:T(8,128)(2,1)} %param.16, bf16[512,4096]{1,0:T(8,128)(2,1)S(1)} %copy-done.1, f32[4096]{0:T(1024)S(1)} %convert_element_type.44, f32[512]{0:T(512)S(1)} %add_rsqrt_fusion.1), kind=kOutput, calls=%fused_computation.37 | convolution fusion | flops 2156134400 | bytes 8931328 | tf_op jit(solution)/shard_map/dot_general | solution.py:39
  286.0 71.1 %all-gather.6.cloned.1.call-done = bf16[48,128,1024]{2,1,0:T(8,128)(2,1)} async-done(((bf16[12,128,1024]{2,1,0:T(8,128)(2,1)}), bf16[48,128,1024]{2,1,0:T(8,128)(2,1)}) %all-gather.6.cloned.1.call-update) | async-done | bytes 12582928 | tf_op jit(solution)/shard_map/all_gather | solution.py:51
  357.1 7.3 %gather_fusion = bf16[16,128,1024]{2,1,0:T(8,128)(2,1)} fusion(bf16[48,128,1024]{2,1,0:T(8,128)(2,1)} %all-gather.6.cloned.1.call-done, s32[1024]{0:T(1024)S(1)} %pad_clamp_fusion), kind=kCustom, calls=%fused_computation | custom fusion | bytes 8388672 | tf_op jit(solution)/shard_map/jit(_take)/gather | solution.py:54
  364.5 7.7 %reshape.75 = bf16[8,256,2,4,128]{4,3,2,1,0:T(4,128)(2,1)} reshape(bf16[16,128,1024]{2,1,0:T(8,128)(2,1)} %gather_fusion) | data formatting | bytes 8388608 | tf_op jit(solution)/shard_map/jit(_take)/gather | solution.py:54
  372.2 2.9 fusion.17
  378.6 5.2 %fusion.27 = bf16[8,64,4,128]{3,1,2,0:T(8,128)(2,1)S(1)} fusion(bf16[8,256,2,4,128]{4,1,3,0,2:T(8,128)(2,1)} %copy-done, f32[8,4,64]{2,1,0:T(4,128)S(1)} %fusion.41, f32[8,4,64,256]{3,2,1,0:T(8,128)S(1)} %fusion.21), kind=kOutput, calls=%fused_computation.38 | convolution fusion | flops 136579328 | bytes 4726784 | tf_op jit(solution)/shard_map/chqk,ckhd->cqhd/dot_general | solution.py:62
  384.3 6.5 %convolution_convert_fusion.1 = bf16[512,4096]{1,0:T(8,128)(2,1)} fusion(bf16[512,4096]{1,0:T(8,128)(2,1)} %param.19, bf16[64,8,4,128]{3,2,1,0:T(4,128)(2,1)S(1)} %bitcast.44), kind=kOutput, calls=%fused_computation.22 | convolution fusion | flops 2149580800 | bytes 8912896 | tf_op jit(solution)/shard_map/dot_general | solution.py:67
  390.8 88.5 %reduce-scatter.2.cloned.1.call-done = bf16[64,4096]{1,0:T(8,128)(2,1)} async-done(((bf16[512,4096]{1,0:T(8,128)(2,1)}), bf16[64,4096]{1,0:T(8,128)(2,1)}) %reduce-scatter.2.cloned.1.call-update) | async-done | bytes 524304 | tf_op jit(solution)/shard_map/reduce_scatter | solution.py:66
  (75 shorter events, 25.2 us)
Async XLA Ops:
  6.5 181.8 %all-gather.4.cloned.1.call-start = ((), (), s32[]{:S(2)}) async-start(), calls=%async_computation.1 | async-start | bytes 14155776 | tf_op jit(solution)/shard_map/all_gather | solution.py:37
  7.3 270.0 %all-gather.8.cloned.1.call-start = ((), (), s32[]{:S(2)}) async-start(), calls=%async_computation.3 | async-start | bytes 4718592 | tf_op jit(solution)/shard_map/all_gather | solution.py:38
  8.0 349.1 %all-gather.6.cloned.1.call-start = ((), (), s32[]{:S(2)}) async-start(), calls=%async_computation.2 | async-start | bytes 15728640 | tf_op jit(solution)/shard_map/all_gather | solution.py:51
  8.1 180.3 %copy-start.2 = (bf16[4096]{0:T(1024)(128)(2,1)S(1)}, bf16[4096]{0:T(1024)(128)(2,1)}, u32[]{:S(2)}) copy-start(bf16[4096]{0:T(1024)(128)(2,1)} %param.15) | copy-start | bytes 24580
  188.4 88.2 %copy-start.4 = (s32[8,2]{0,1:T(2,128)S(1)}, s32[8,2]{0,1:T(2,128)}, u32[]{:S(2)}) copy-start(s32[8,2]{0,1:T(2,128)} %param.21) | copy-start | bytes 196
  188.4 88.4 %copy-start.5 = (s32[16,1]{0,1:T(1,128)S(1)}, s32[16,1]{0,1:T(1,128)}, u32[]{:S(2)}) copy-start(s32[16,1]{0,1:T(1,128)} %param.20) | copy-start | bytes 196
  188.4 88.8 %copy-start.3 = (bf16[4096]{0:T(1024)(128)(2,1)S(1)}, bf16[4096]{0:T(1024)(128)(2,1)}, u32[]{:S(2)}) copy-start(bf16[4096]{0:T(1024)(128)(2,1)} %param.13) | copy-start | bytes 24580
  276.3 202.9 %reduce-scatter.2.cloned.1.call-start = ((), (), s32[]{:S(2)}) async-start(), calls=%async_computation.4 | async-start | bytes 4718592 | tf_op jit(solution)/shard_map/reduce_scatter | solution.py:66
  277.3 3.5 copy-start.1
  375.1 1.9 copy-start
Sparse Core Ops, SparseCore 0:
  9.5 178.8 all-gather.3
  190.4 72.8 all-gather.7
  276.5 80.6 all-gather.5
  390.9 88.3 reduce-scatter.1
where the time goes:
time: 487 us; the launch traced here: 486 us
  waiting for transfers between devices  333 us (68%)
  matrix products  87.1 us (18%)
  other arithmetic  33.3 us (7%)
  local copies, waits for them, and re-layouts  18.3 us (4%)
  between operations  13.2 us (3%)
    all_gather x1, waiting for transfers between devices, per_device(): lax.all_gather(nbr_tokens, 'enc', axis=1, tiled=True)  172 us
    reduce_scatter x1, waiting for transfers between devices, per_device(): lax.psum_scatter(jnp.dot(context, out_weight, preferred_element_type=jnp....  88.5 us
    all_gather x1, waiting for transfers between devices, per_device(): piece = lax.all_gather(encoded, 'dp', axis=0, tiled=True)  71.1 us
    dot_general x12, matrix products, encode_tile(): jnp.dot(normalize(tile, enc_gain), kv_weight, preferred_element_type=jnp....  69.4 us
    reduce_sum x13, other arithmetic, normalize(): scale = lax.rsqrt(jnp.mean(values * values, axis=-1, keepdims=True) + 1e-05)  21.6 us
    gather x2, local copies, waits for them, and re-layouts, per_device(): picked = jnp.take(piece, jnp.clip(tile_ids, 0, count - 1), axis=0)  15.1 us
  transfers between devices with their start and end apart: 4, of which 3 were waited for; matrix products, arithmetic and copies ran while one was open for 22% of the time, Pallas kernels for 0%

commit v1 on v0

--- a/solution.py
+++ b/solution.py
@@ -7,6 +7,27 @@
 SPAN = 64
 NL = 128
 NBRS = 2
+
+
+def collect(value, axis, dim):
+    count, position, span = (lax.axis_size(axis), lax.axis_index(axis), value.shape[dim])
+    right = [(i, (i + 1) % count) for i in range(count)]
+    backward = [(i, (i - 1) % count) for i in range(count)]
+    result = jnp.zeros((*value.shape[:dim], count * span, *value.shape[dim + 1 :]), value.dtype)
+    result = lax.dynamic_update_slice_in_dim(result, value, position * span, axis=dim)
+    from_left = from_right = value
+    half = count // 2
+    for step in range(1, half + 1):
+        from_left = lax.ppermute(from_left, axis, right)
+        result = lax.dynamic_update_slice_in_dim(
+            result, from_left, (position - step) % count * span, axis=dim
+        )
+        if step < count - half:
+            from_right = lax.ppermute(from_right, axis, backward)
+            result = lax.dynamic_update_slice_in_dim(
+                result, from_right, (position + step) % count * span, axis=dim
+            )
+    return result
 
 
 def normalize(rows, gain):
@@ -48,7 +69,7 @@
     tiles_dev = encoded.shape[0]
     tile_ids = owners * tiles_dev + tile_local
     empty = jnp.zeros((owners.shape[0],) + encoded.shape[1:], jnp.bfloat16)
-    piece = lax.all_gather(encoded, "dp", axis=0, tiled=True)
+    piece = collect(encoded, "dp", 0)
     count = piece.shape[0]
     inside = (tile_ids >= 0) & (tile_ids < count)
     picked = jnp.take(piece, jnp.clip(tile_ids, 0, count - 1), axis=0)

time: 487 us -> 515 us (1.057)
  local copies, waits for them, and re-layouts: 18.3 us -> 38.3 us
  waiting for transfers between devices: 333 us -> 340 us
    ppermute x0 -> x3, waiting for transfers between devices: none -> 77.8 us  [the longest x2 77.8 us: collect(): from_left = lax.ppermute(from_left, axis, right)]
    all_gather x1 -> x0, waiting for transfers between devices: 71.1 us -> none  [per_device(): piece = lax.all_gather(encoded, 'dp', axis=0, tiled=True)]
    dynamic_update_slice x0 -> x4, local copies, waits for them, and re-layouts: none -> 12 us  [the longest x2 6.09 us: collect(): lax.dynamic_update_slice_in_dim(result, from_left, (position - step) % co...]
    broadcast_in_dim x0 -> x1, local copies, waits for them, and re-layouts: none -> 6.18 us  [collect(): jnp.zeros((*value.shape[:dim], count * span, *value.shape[dim + 1:]), val...]
  transfers between devices with their start and end apart: 4 -> 6, of which waited for: 3 -> 4; matrix products, arithmetic and copies ran while one was open for 22% -> 24% of each run, Pallas kernels for 0% -> 0%
where the time goes in v1:
time: 515 us; the launch traced here: 514 us
  waiting for transfers between devices  340 us (66%)
  matrix products  87.3 us (17%)
  local copies, waits for them, and re-layouts  38.3 us (7%)
  other arithmetic  33.4 us (6%)
  between operations  13.2 us (3%)
    all_gather x1, waiting for transfers between devices, per_device(): lax.all_gather(nbr_tokens, 'enc', axis=1, tiled=True)  172 us
    reduce_scatter x1, waiting for transfers between devices, per_device(): lax.psum_scatter(jnp.dot(context, out_weight, preferred_element_type=jnp....  87.9 us
    ppermute x2, waiting for transfers between devices, collect(): from_left = lax.ppermute(from_left, axis, right)  77.8 us
    dot_general x12, matrix products, encode_tile(): jnp.dot(normalize(tile, enc_gain), kv_weight, preferred_element_type=jnp....  69.4 us
    reduce_sum x13, other arithmetic, normalize(): scale = lax.rsqrt(jnp.mean(values * values, axis=-1, keepdims=True) + 1e-05)  21.6 us
    gather x2, local copies, waits for them, and re-layouts, per_device(): picked = jnp.take(piece, jnp.clip(tile_ids, 0, count - 1), axis=0)  15.1 us
  transfers between devices with their start and end apart: 6, of which 4 were waited for; matrix products, arithmetic and copies ran while one was open for 24% of the time, Pallas kernels for 0%

profile of v1, /device:TPU:0, one launch (start us, length us, event | category | flops | bytes accessed | tf_op | source)
XLA Modules:
  0.0 514.0 jit_solution(15262113475918379012)
XLA Ops:
  8.1 7.8 %pad_maximum_fusion = bf16[4096,1024]{1,0:T(8,128)(2,1)} fusion(bf16[4096,512]{1,0:T(8,128)(2,1)} %param.18, bf16[4096,512]{1,0:T(8,128)(2,1)} %param.17), kind=kLoop, calls=%fused_computation.21 | loop fusion | flops 16777216 | bytes 16777216 | tf_op jit(solution)/shard_map/concatenate | solution.py:51
  15.9 172.5 %all-gather.3.cloned.1.call-done = bf16[12,128,4096]{2,1,0:T(8,128)(2,1)} async-done(((bf16[12,16,4096]{2,1,0:T(8,128)(2,1)}), bf16[12,128,4096]{2,1,0:T(8,128)(2,1)}) %all-gather.3.cloned.1.call-update) | async-done | bytes 12582928 | tf_op jit(solution)/shard_map/all_gather | solution.py:58
  188.4 88.0 %while.10 = (s32[]{:T(128)}, bf16[12,128,1024]{2,1,0:T(8,128)(2,1)}, bf16[12,128,4096]{2,1,0:T(8,128)(2,1)}, bf16[4096]{0:T(1024)(128)(2,1)S(1)}, bf16[4096,1024]{1,0:T(8,128)(2,1)}, /*index=5*/s32[]{:T(128)}) while((s32[]{:T(128)}, bf16[12,128,1024]{2,1,0:T(8,128)(2,1)}, bf16[12,128,4096]{2,1,0:T(8,128)(2,1)}, bf16[4096]{0:T(1024)(128)(2,1)S(1)}, ...), condition=%wide.region_2.3_spmd, body=%wide.region_0.2_spmd.sunk | while | flops 1077547136 | bytes 10792009 | solution.py:58
  190.0 5.7 %fusion.52 = bf16[12,128,1024]{2,1,0:T(8,128)(2,1)} fusion(bf16[12,128,1024]{2,1,0:T(8,128)(2,1)} %get-tuple-element.85, s32[]{:T(128)} %get-tuple-element.84, bf16[4096,1024]{1,0:T(8,128)(2,1)} %get-tuple-element.94, f32[4096]{0:T(1024)S(1)} %convert_element_type.86, f32[128]{0:T(128)S(1)} %add_rsqrt_fusion.3, ...), kind=kOutput, calls=%fused_computation.8.clone.1 | convolution fusion | flops 1075970048 | bytes 9717248 | tf_op jit(solution)/shard_map/while/body/eval_jaxpr/dot_general | solution.py:54
  197.3 5.8 %fusion.52 = bf16[12,128,1024]{2,1,0:T(8,128)(2,1)} fusion(bf16[12,128,1024]{2,1,0:T(8,128)(2,1)} %get-tuple-element.85, s32[]{:T(128)} %get-tuple-element.84, bf16[4096,1024]{1,0:T(8,128)(2,1)} %get-tuple-element.94, f32[4096]{0:T(1024)S(1)} %convert_element_type.86, f32[128]{0:T(128)S(1)} %add_rsqrt_fusion.3, ...), kind=kOutput, calls=%fused_computation.8.clone.1 | convolution fusion | flops 1075970048 | bytes 9717248 | tf_op jit(solution)/shard_map/while/body/eval_jaxpr/dot_general | solution.py:54
  204.7 5.8 %fusion.52 = bf16[12,128,1024]{2,1,0:T(8,128)(2,1)} fusion(bf16[12,128,1024]{2,1,0:T(8,128)(2,1)} %get-tuple-element.85, s32[]{:T(128)} %get-tuple-element.84, bf16[4096,1024]{1,0:T(8,128)(2,1)} %get-tuple-element.94, f32[4096]{0:T(1024)S(1)} %convert_element_type.86, f32[128]{0:T(128)S(1)} %add_rsqrt_fusion.3, ...), kind=kOutput, calls=%fused_computation.8.clone.1 | convolution fusion | flops 1075970048 | bytes 9717248 | tf_op jit(solution)/shard_map/while/body/eval_jaxpr/dot_general | solution.py:54
  212.0 5.8 %fusion.52 = bf16[12,128,1024]{2,1,0:T(8,128)(2,1)} fusion(bf16[12,128,1024]{2,1,0:T(8,128)(2,1)} %get-tuple-element.85, s32[]{:T(128)} %get-tuple-element.84, bf16[4096,1024]{1,0:T(8,128)(2,1)} %get-tuple-element.94, f32[4096]{0:T(1024)S(1)} %convert_element_type.86, f32[128]{0:T(128)S(1)} %add_rsqrt_fusion.3, ...), kind=kOutput, calls=%fused_computation.8.clone.1 | convolution fusion | flops 1075970048 | bytes 9717248 | tf_op jit(solution)/shard_map/while/body/eval_jaxpr/dot_general | solution.py:54
  219.4 5.7 %fusion.52 = bf16[12,128,1024]{2,1,0:T(8,128)(2,1)} fusion(bf16[12,128,1024]{2,1,0:T(8,128)(2,1)} %get-tuple-element.85, s32[]{:T(128)} %get-tuple-element.84, bf16[4096,1024]{1,0:T(8,128)(2,1)} %get-tuple-element.94, f32[4096]{0:T(1024)S(1)} %convert_element_type.86, f32[128]{0:T(128)S(1)} %add_rsqrt_fusion.3, ...), kind=kOutput, calls=%fused_computation.8.clone.1 | convolution fusion | flops 1075970048 | bytes 9717248 | tf_op jit(solution)/shard_map/while/body/eval_jaxpr/dot_general | solution.py:54
  226.7 5.9 %fusion.52 = bf16[12,128,1024]{2,1,0:T(8,128)(2,1)} fusion(bf16[12,128,1024]{2,1,0:T(8,128)(2,1)} %get-tuple-element.85, s32[]{:T(128)} %get-tuple-element.84, bf16[4096,1024]{1,0:T(8,128)(2,1)} %get-tuple-element.94, f32[4096]{0:T(1024)S(1)} %convert_element_type.86, f32[128]{0:T(128)S(1)} %add_rsqrt_fusion.3, ...), kind=kOutput, calls=%fused_computation.8.clone.1 | convolution fusion | flops 1075970048 | bytes 9717248 | tf_op jit(solution)/shard_map/while/body/eval_jaxpr/dot_general | solution.py:54
  234.1 5.8 %fusion.52 = bf16[12,128,1024]{2,1,0:T(8,128)(2,1)} fusion(bf16[12,128,1024]{2,1,0:T(8,128)(2,1)} %get-tuple-element.85, s32[]{:T(128)} %get-tuple-element.84, bf16[4096,1024]{1,0:T(8,128)(2,1)} %get-tuple-element.94, f32[4096]{0:T(1024)S(1)} %convert_element_type.86, f32[128]{0:T(128)S(1)} %add_rsqrt_fusion.3, ...), kind=kOutput, calls=%fused_computation.8.clone.1 | convolution fusion | flops 1075970048 | bytes 9717248 | tf_op jit(solution)/shard_map/while/body/eval_jaxpr/dot_general | solution.py:54
  241.4 5.7 %fusion.52 = bf16[12,128,1024]{2,1,0:T(8,128)(2,1)} fusion(bf16[12,128,1024]{2,1,0:T(8,128)(2,1)} %get-tuple-element.85, s32[]{:T(128)} %get-tuple-element.84, bf16[4096,1024]{1,0:T(8,128)(2,1)} %get-tuple-element.94, f32[4096]{0:T(1024)S(1)} %convert_element_type.86, f32[128]{0:T(128)S(1)} %add_rsqrt_fusion.3, ...), kind=kOutput, calls=%fused_computation.8.clone.1 | convolution fusion | flops 1075970048 | bytes 9717248 | tf_op jit(solution)/shard_map/while/body/eval_jaxpr/dot_general | solution.py:54
  248.7 5.9 %fusion.52 = bf16[12,128,1024]{2,1,0:T(8,128)(2,1)} fusion(bf16[12,128,1024]{2,1,0:T(8,128)(2,1)} %get-tuple-element.85, s32[]{:T(128)} %get-tuple-element.84, bf16[4096,1024]{1,0:T(8,128)(2,1)} %get-tuple-element.94, f32[4096]{0:T(1024)S(1)} %convert_element_type.86, f32[128]{0:T(128)S(1)} %add_rsqrt_fusion.3, ...), kind=kOutput, calls=%fused_computation.8.clone.1 | convolution fusion | flops 1075970048 | bytes 9717248 | tf_op jit(solution)/shard_map/while/body/eval_jaxpr/dot_general | solution.py:54
  256.1 5.7 %fusion.52 = bf16[12,128,1024]{2,1,0:T(8,128)(2,1)} fusion(bf16[12,128,1024]{2,1,0:T(8,128)(2,1)} %get-tuple-element.85, s32[]{:T(128)} %get-tuple-element.84, bf16[4096,1024]{1,0:T(8,128)(2,1)} %get-tuple-element.94, f32[4096]{0:T(1024)S(1)} %convert_element_type.86, f32[128]{0:T(128)S(1)} %add_rsqrt_fusion.3, ...), kind=kOutput, calls=%fused_computation.8.clone.1 | convolution fusion | flops 1075970048 | bytes 9717248 | tf_op jit(solution)/shard_map/while/body/eval_jaxpr/dot_general | solution.py:54
  263.4 5.7 %fusion.52 = bf16[12,128,1024]{2,1,0:T(8,128)(2,1)} fusion(bf16[12,128,1024]{2,1,0:T(8,128)(2,1)} %get-tuple-element.85, s32[]{:T(128)} %get-tuple-element.84, bf16[4096,1024]{1,0:T(8,128)(2,1)} %get-tuple-element.94, f32[4096]{0:T(1024)S(1)} %convert_element_type.86, f32[128]{0:T(128)S(1)} %add_rsqrt_fusion.3, ...), kind=kOutput, calls=%fused_computation.8.clone.1 | convolution fusion | flops 1075970048 | bytes 9717248 | tf_op jit(solution)/shard_map/while/body/eval_jaxpr/dot_general | solution.py:54
  270.7 5.7 %fusion.52 = bf16[12,128,1024]{2,1,0:T(8,128)(2,1)} fusion(bf16[12,128,1024]{2,1,0:T(8,128)(2,1)} %get-tuple-element.85, s32[]{:T(128)} %get-tuple-element.84, bf16[4096,1024]{1,0:T(8,128)(2,1)} %get-tuple-element.94, f32[4096]{0:T(1024)S(1)} %convert_element_type.86, f32[128]{0:T(128)S(1)} %add_rsqrt_fusion.3, ...), kind=kOutput, calls=%fused_computation.8.clone.1 | convolution fusion | flops 1075970048 | bytes 9717248 | tf_op jit(solution)/shard_map/while/body/eval_jaxpr/dot_general | solution.py:54
  278.1 67.0 %collective-permute-done = bf16[12,128,1024]{2,1,0:T(8,128)(2,1)S(1)} collective-permute-done((bf16[12,128,1024]{2,1,0:T(8,128)(2,1)}, bf16[12,128,1024]{2,1,0:T(8,128)(2,1)S(1)}, u32[]{:S(2)}, u32[]{:S(2)}) %collective-permute-start) | collective-permute-done | bytes 3145760 | tf_op jit(solution)/shard_map/ppermute | solution.py:21
  349.6 5.4 %fusion.24 = bf16[512,512]{1,0:T(8,128)(2,1)} fusion(bf16[4096,512]{1,0:T(8,128)(2,1)} %param.16, bf16[512,4096]{1,0:T(8,128)(2,1)S(1)} %copy-done.1, f32[4096]{0:T(1024)S(1)} %convert_element_type.44, f32[512]{0:T(512)S(1)} %add_rsqrt_fusion.1), kind=kOutput, calls=%fused_computation.37 | convolution fusion | flops 2156134400 | bytes 8931328 | tf_op jit(solution)/shard_map/dot_general | solution.py:60
  356.9 6.2 %broadcast_in_dim.55 = bf16[48,128,1024]{2,1,0:T(8,128)(2,1)} broadcast(bf16[]{:T(256)} %constant.75.clone.1), dimensions={} | broadcast | bytes 12582914 | tf_op jit(solution)/shard_map/broadcast_in_dim | solution.py:16
  371.2 10.8 %collective-permute-done.2 = bf16[12,128,1024]{2,1,0:T(8,128)(2,1)} collective-permute-done((bf16[12,128,1024]{2,1,0:T(8,128)(2,1)S(1)}, bf16[12,128,1024]{2,1,0:T(8,128)(2,1)}, u32[]{:S(2)}, u32[]{:S(2)}) %collective-permute-start.2) | collective-permute-done | bytes 3145760 | tf_op jit(solution)/shard_map/ppermute | solution.py:21
  385.9 7.3 %gather_fusion = bf16[16,128,1024]{2,1,0:T(8,128)(2,1)} fusion(bf16[48,128,1024]{2,1,0:T(8,128)(2,1)} %constant_dynamic-update-slice_fusion, s32[1024]{0:T(1024)S(1)} %pad_clamp_fusion), kind=kCustom, calls=%fused_computation | custom fusion | bytes 8388672 | tf_op jit(solution)/shard_map/jit(_take)/gather | solution.py:75
  393.2 7.7 %reshape.75 = bf16[8,256,2,4,128]{4,3,2,1,0:T(4,128)(2,1)} reshape(bf16[16,128,1024]{2,1,0:T(8,128)(2,1)} %gather_fusion) | data formatting | bytes 8388608 | tf_op jit(solution)/shard_map/jit(_take)/gather | solution.py:75
  407.4 5.2 %fusion.27 = bf16[8,64,4,128]{3,1,2,0:T(8,128)(2,1)S(1)} fusion(bf16[8,256,2,4,128]{4,1,3,0,2:T(8,128)(2,1)} %copy-done, f32[8,4,64]{2,1,0:T(4,128)S(1)} %fusion.41, f32[8,4,64,256]{3,2,1,0:T(8,128)S(1)} %fusion.21), kind=kOutput, calls=%fused_computation.38 | convolution fusion | flops 136579328 | bytes 4726784 | tf_op jit(solution)/shard_map/chqk,ckhd->cqhd/dot_general | solution.py:83
  413.1 6.5 %convolution_convert_fusion.1 = bf16[512,4096]{1,0:T(8,128)(2,1)} fusion(bf16[512,4096]{1,0:T(8,128)(2,1)} %param.19, bf16[64,8,4,128]{3,2,1,0:T(4,128)(2,1)S(1)} %bitcast.44), kind=kOutput, calls=%fused_computation.22 | convolution fusion | flops 2149580800 | bytes 8912896 | tf_op jit(solution)/shard_map/dot_general | solution.py:88
  419.6 87.9 %reduce-scatter.2.cloned.1.call-done = bf16[64,4096]{1,0:T(8,128)(2,1)} async-done(((bf16[512,4096]{1,0:T(8,128)(2,1)}), bf16[64,4096]{1,0:T(8,128)(2,1)}) %reduce-scatter.2.cloned.1.call-update) | async-done | bytes 524304 | tf_op jit(solution)/shard_map/reduce_scatter | solution.py:87
  (87 shorter events, 47.0 us)
Async XLA Ops:
  6.5 181.8 %all-gather.3.cloned.1.call-start = ((), (), s32[]{:S(2)}) async-start(), calls=%async_computation.1 | async-start | bytes 14155776 | tf_op jit(solution)/shard_map/all_gather | solution.py:58
  7.3 338.9 %all-gather.5.cloned.1.call-start = ((), (), s32[]{:S(2)}) async-start(), calls=%async_computation.2 | async-start | bytes 4718592 | tf_op jit(solution)/shard_map/all_gather | solution.py:59
  8.0 499.4 %reduce-scatter.2.cloned.1.call-start = ((), (), s32[]{:S(2)}) async-start(), calls=%async_computation.3 | async-start | bytes 4718592 | tf_op jit(solution)/shard_map/reduce_scatter | solution.py:87
  8.1 180.3 %copy-start.4 = (bf16[4096]{0:T(1024)(128)(2,1)S(1)}, bf16[4096]{0:T(1024)(128)(2,1)}, u32[]{:S(2)}) copy-start(bf16[4096]{0:T(1024)(128)(2,1)} %param.15) | copy-start | bytes 24580
  188.4 157.1 %copy-start.6 = (s32[8,2]{0,1:T(2,128)S(1)}, s32[8,2]{0,1:T(2,128)}, u32[]{:S(2)}) copy-start(s32[8,2]{0,1:T(2,128)} %param.21) | copy-start | bytes 196
  188.4 157.3 %copy-start.7 = (s32[16,1]{0,1:T(1,128)S(1)}, s32[16,1]{0,1:T(1,128)}, u32[]{:S(2)}) copy-start(s32[16,1]{0,1:T(1,128)} %param.20) | copy-start | bytes 196
  188.4 157.7 %copy-start.5 = (bf16[4096]{0:T(1024)(128)(2,1)S(1)}, bf16[4096]{0:T(1024)(128)(2,1)}, u32[]{:S(2)}) copy-start(bf16[4096]{0:T(1024)(128)(2,1)} %param.13) | copy-start | bytes 24580
  276.4 68.8 %collective-permute-start = (bf16[12,128,1024]{2,1,0:T(8,128)(2,1)}, bf16[12,128,1024]{2,1,0:T(8,128)(2,1)S(1)}, u32[]{:S(2)}, u32[]{:S(2)}) collective-permute-start(bf16[12,128,1024]{2,1,0:T(8,128)(2,1)} %get-tuple-element.32), channel_id=1, source_target_pairs={{0,8},{8,16},{16,24},{24,0},{1,9},{9,17},{17,25},{25,1},{2,10},{10... | collective-permute-start | bytes 9437192 | tf_op jit(solution)/shard_map/ppermute | solution.py:21
  276.4 90.9 %collective-permute-start.1 = (bf16[12,128,1024]{2,1,0:T(8,128)(2,1)}, bf16[12,128,1024]{2,1,0:T(8,128)(2,1)}, u32[]{:S(2)}, u32[]{:S(2)}) collective-permute-start(bf16[12,128,1024]{2,1,0:T(8,128)(2,1)} %get-tuple-element.32), channel_id=1, source_target_pairs={{0,24},{8,0},{16,8},{24,16},{1,25},{9,1},{17,9},{25,17},{2,26},{10... | collective-permute-start | bytes 9437192 | tf_op jit(solution)/shard_map/ppermute | solution.py:26
  345.2 36.8 %collective-permute-start.2 = (bf16[12,128,1024]{2,1,0:T(8,128)(2,1)S(1)}, bf16[12,128,1024]{2,1,0:T(8,128)(2,1)}, u32[]{:S(2)}, u32[]{:S(2)}) collective-permute-start(bf16[12,128,1024]{2,1,0:T(8,128)(2,1)S(1)} %collective-permute-done), channel_id=1, source_target_pairs={{0,8},{8,16},{16,24},{24,0},{1,9},{9,17},{17,25},{25,1},{2,10},{10... | collective-permute-start | bytes 9437192 | tf_op jit(solution)/shard_map/ppermute | solution.py:21
  346.2 3.5 copy-start.1
  356.9 6.2 %copy-start.2 = (bf16[12,128,1024]{2,1,0:T(8,128)(2,1)S(1)}, bf16[12,128,1024]{2,1,0:T(8,128)(2,1)}, u32[]{:S(2)}) copy-start(bf16[12,128,1024]{2,1,0:T(8,128)(2,1)} %get-tuple-element.32) | copy-start | bytes 9437188
  400.9 4.9 copy-start.3
  403.9 1.9 copy-start
Sparse Core Ops, SparseCore 0:
  9.5 178.8 all-gather.2
  190.4 72.8 all-gather.4
  419.7 87.7 reduce-scatter.1
